TPU v7x, 128 devices: a whole 4x4x4 slice. The times are simulated.
128 devices in a mesh: dp: 16 (over x, y), tensor: 8 (over z, core).
Axes of the slice: x: 4, y: 4, z: 4, core: 2. Of those that a mesh axis runs over, the one named last changes fastest.
Arguments:
- kv_part: bfloat16 [8, 4096, 12288], P('tensor', 'dp'), may hold values from -2 to 2
- queries: bfloat16 [8192, 6144], P('dp', 'tensor'), may hold values from -6 to 6
- w_out: bfloat16 [6144, 8192], P('tensor'), may hold values from -0.078125 to 0.078125
- d_out: bfloat16 [8192, 8192], P('dp', 'tensor'), may hold values from -48 to 48
- nbr_owner: int32 [128, 2], replicated, may hold values from 0 to 15, as said below
- nbr_slot: int32 [128, 2], replicated, may hold values from 0 to 1, as said below
Outputs:
- mixed: bfloat16 [8192, 8192], P('dp', 'tensor')
- d_kv: bfloat16 [4096, 12288], P('dp', 'tensor')
Inputs may be any that keep to these rules, and one draw needn't show every extreme that they name: `nbr_owner`: the two neighbours of one span have different owners. `nbr_slot`: all neighbours that the spans of one dp index r (spans r * 8 to (r + 1) * 8 - 1) take from one owner have the same slot.
All inputs are finite; a program needn't handle non-finite values.
Results may differ from a plain program's by a relative error of at most 0.025.
Values may be sent and summed in bfloat16 or wider, within the bound.
A program may use at most 192 MiB of HBM per device.

v0:
```python
import jax
import jax.numpy as jnp
from jax import lax
from jax.sharding import PartitionSpec as P

HD = 128
SPAN = 64
NBR_LEN = 128
NB_DEV = 2


def local(kv_part, queries, w_out, d_out, nbr_owner, nbr_slot):
    dp_count = lax.axis_size("dp")
    reader = lax.axis_index("dp")
    head_width = w_out.shape[0]
    heads_here = head_width // HD
    share_width = 2 * head_width
    span_count = queries.shape[0] // SPAN
    read_count = 2 * span_count
    block_width = NBR_LEN * share_width
    local_partial = kv_part[0]
    summed = lax.psum(local_partial, "tensor").astype(jnp.float32)
    shares = lax.dynamic_slice_in_dim(
        summed, lax.axis_index("tensor") * share_width, share_width, 1
    ).astype(jnp.bfloat16)
    share_blocks = shares.reshape(NB_DEV, block_width)
    owner_ids = jnp.arange(dp_count, dtype=jnp.int32)
    slot_ids = jnp.arange(NB_DEV, dtype=jnp.int32)
    owner_hits = nbr_owner[:, :, None] == owner_ids[None, None, :]
    per_reader = owner_hits.reshape(dp_count, read_count, dp_count)
    reads_from = jnp.any(per_reader, axis=1)
    slot_from = jnp.max(jnp.where(per_reader, nbr_slot.reshape(dp_count, read_count, 1), 0), axis=1)
    my_owner = lax.dynamic_slice_in_dim(nbr_owner, reader * span_count, span_count, 0).reshape(
        read_count
    )
    my_slot = lax.dynamic_slice_in_dim(nbr_slot, reader * span_count, span_count, 0).reshape(
        read_count
    )
    read_table = (my_owner[:, None] == owner_ids[None, :]).astype(jnp.bfloat16)
    serving = lax.dynamic_index_in_dim(reads_from, reader, 1, False)
    serving_slot = lax.dynamic_index_in_dim(slot_from, reader, 1, False)
    owner_select = ((serving_slot[:, None] == slot_ids[None, :]) & serving[:, None]).astype(
        jnp.bfloat16
    )
    everyone = lax.all_gather(share_blocks, "dp", axis=0, tiled=True)
    wanted = (my_owner * NB_DEV + my_slot)[:, None] == jnp.arange(
        dp_count * NB_DEV, dtype=jnp.int32
    )[None, :]
    neighbours = jnp.dot(
        wanted.astype(jnp.bfloat16), everyone, preferred_element_type=jnp.float32
    ).astype(jnp.bfloat16)
    layout = neighbours.reshape(span_count, 2 * NBR_LEN, heads_here, 2, HD)
    keys = layout[:, :, :, 0]
    values = layout[:, :, :, 1]
    query_view = queries.reshape(span_count, SPAN, heads_here, HD)
    factor = HD ** (-0.5)
    scores = (
        jnp.einsum("cqhd,ckhd->chqk", query_view, keys, preferred_element_type=jnp.float32) * factor
    )
    highest = jnp.max(scores, axis=-1, keepdims=True)
    expo = jnp.exp(scores - highest)
    probs = expo / jnp.sum(expo, axis=-1, keepdims=True)
    probs_low = probs.astype(jnp.bfloat16)
    attended = jnp.einsum("chqk,ckhd->cqhd", probs_low, values, preferred_element_type=jnp.float32)
    attended = attended.astype(jnp.bfloat16).reshape(span_count * SPAN, head_width)
    partial_out = jnp.dot(attended, w_out, preferred_element_type=jnp.float32)
    mixed = lax.psum_scatter(
        partial_out.astype(jnp.bfloat16), "tensor", scatter_dimension=1, tiled=True
    )
    grad_attended = lax.dot_general(
        lax.all_gather(d_out, "tensor", axis=1, tiled=True),
        w_out,
        (((1,), (1,)), ((), ())),
        preferred_element_type=jnp.float32,
    ).astype(jnp.bfloat16)
    grad_view = grad_attended.reshape(span_count, SPAN, heads_here, HD)
    grad_values = jnp.einsum(
        "chqk,cqhd->ckhd", probs_low, grad_view, preferred_element_type=jnp.float32
    )
    grad_probs = jnp.einsum(
        "cqhd,ckhd->chqk", grad_view, values, preferred_element_type=jnp.float32
    )
    grad_scores = probs * (grad_probs - jnp.sum(probs * grad_probs, axis=-1, keepdims=True))
    grad_scores = grad_scores.astype(jnp.bfloat16)
    grad_keys = (
        jnp.einsum("chqk,cqhd->ckhd", grad_scores, query_view, preferred_element_type=jnp.float32)
        * factor
    )
    grad_blocks = jnp.stack([grad_keys, grad_values], axis=3).reshape(read_count, block_width)
    per_owner = lax.dot_general(
        read_table.astype(jnp.float32),
        grad_blocks,
        (((0,), (0,)), ((), ())),
        precision=lax.Precision.HIGHEST,
        preferred_element_type=jnp.float32,
    ).astype(jnp.bfloat16)
    returned = lax.all_to_all(per_owner, "dp", split_axis=0, concat_axis=0, tiled=True)
    owner_grad = lax.dot_general(
        owner_select, returned, (((0,), (0,)), ((), ())), preferred_element_type=jnp.float32
    )
    d_kv = owner_grad.astype(jnp.bfloat16).reshape(NB_DEV * NBR_LEN, share_width)
    return (mixed, d_kv)


def solution(mesh):
    placed = (
        P("tensor", "dp", None),
        P("dp", "tensor"),
        P("tensor", None),
        P("dp", "tensor"),
        P(),
        P(),
    )
    return jax.shard_map(
        local,
        mesh=mesh,
        in_specs=placed,
        out_specs=(P("dp", "tensor"), P("dp", "tensor")),
        check_vma=False,
    )
```

profile of v0, /device:TPU:28, one launch (start us, length us, event | category | flops | bytes accessed | tf_op | source)
XLA Modules:
  0.0 541.4 jit_solution(5792027820581872935)
XLA Ops:
  7.2 0.7 all-reduce.2.cloned.1.call-update
  7.9 0.0 all-gather.6.cloned.1.call-start
  8.0 89.0 %all-reduce.2.cloned.1.call-done = bf16[256,12288]{1,0:T(8,128)(2,1)} async-done(((bf16[256,12288]{1,0:T(8,128)(2,1)}), bf16[256,12288]{1,0:T(8,128)(2,1)}) %all-reduce.2.cloned.1.call-update) | async-done | bytes 6291472 | tf_op jit(solution)/shard_map/psum | solution.py:22
  97.0 1.2 convert_convert_fusion
  98.2 1.5 reshape.62
  99.7 0.0 all-gather.4.cloned.1.call-start
  99.7 0.7 all-gather.4.cloned.1.call-update
  100.5 0.1 constant_dynamic-slice_fusion
  100.5 0.1 copy.73
  100.6 0.1 reshape.54
  100.7 0.1 copy.72
  100.8 0.1 reshape.53
  100.9 1.9 reshape.57
  102.8 85.0 %all-gather.6.cloned.1.call-done = bf16[16,2,196608]{2,1,0:T(2,128)(2,1)} async-done(((bf16[1,2,196608]{2,1,0:T(2,128)(2,1)}), bf16[16,2,196608]{2,1,0:T(2,128)(2,1)}) %all-gather.6.cloned.1.call-update) | async-done | bytes 12582928 | tf_op jit(solution)/shard_map/all_gather | solution.py:45
  187.7 11.3 %reshape.63 = bf16[32,196608]{1,0:T(8,128)(2,1)} reshape(bf16[16,2,196608]{2,1,0:T(2,128)(2,1)} %all-gather.6.cloned.1.call-done) | data formatting | bytes 25165824
  199.0 10.4 %convolution_convert_fusion.1 = bf16[16,196608]{1,0:T(8,128)(2,1)} fusion(bf16[32,196608]{1,0:T(8,128)(2,1)} %reshape.63, s32[16]{0:T(128)S(1)} %multiply_add_fusion), kind=kOutput, calls=%fused_computation.2 | convolution fusion | flops 204472832 | bytes 18874432 | tf_op jit(solution)/shard_map/dot_general | solution.py:49
  209.4 9.9 %reshape.56 = bf16[8,256,6,2,128]{4,3,2,1,0:T(2,128)(2,1)} reshape(bf16[16,196608]{1,0:T(8,128)(2,1)} %convolution_convert_fusion.1) | data formatting | bytes 12582912 | tf_op jit(solution)/shard_map/reshape | solution.py:52
  219.3 13.7 %fusion.42 = (bf16[8,256,6,1,128]{4,3,2,1,0:T(2,128)(2,1)S(1)}, bf16[8,256,6,1,128]{4,3,2,1,0:T(2,128)(2,1)}) fusion(bf16[8,256,6,2,128]{4,3,2,1,0:T(2,128)(2,1)} %reshape.56), kind=kLoop, calls=%fused_computation.54 | loop fusion | bytes 12582912 | tf_op jit(solution)/shard_map/slice | solution.py:53
  233.0 1.2 fusion.4
  234.2 2.3 fusion.43
  236.5 9.2 %fusion.12 = bf16[8,64,6,128]{3,1,2,0:T(8,128)(2,1)} fusion(bf16[8,256,6,1,128]{4,3,2,1,0:T(2,128)(2,1)} %get-tuple-element.3, f32[8,6,64]{2,1,0:T(8,128)S(1)} %get-tuple-element.4, f32[8,6,256,64]{2,3,1,0:T(8,128)S(1)} %fusion.4), kind=kOutput, calls=%fused_computation.27 | convolution fusion | flops 205655296 | bytes 7090176 | tf_op jit(solution)/shard_map/chqk,ckhd->cqhd/dot_general | solution.py:64
  245.7 1.7 copy.77
  247.4 13.4 %convolution_convert_fusion.3 = bf16[512,8192]{1,0:T(8,128)(2,1)} fusion(bf16[768,8192]{1,0:T(8,128)(2,1)} %param.8, bf16[64,8,6,128]{3,2,1,0:T(8,128)(2,1)S(1)} %bitcast.71), kind=kOutput, calls=%fused_computation.6 | convolution fusion | flops 6446645248 | bytes 21757952 | tf_op jit(solution)/shard_map/dot_general | solution.py:66
  260.9 13.5 %convolution_convert_fusion.5 = bf16[512,768]{1,0:T(8,128)(2,1)} fusion(bf16[512,8192]{1,0:T(8,128)(2,1)} %all-gather.4.cloned.1.call-done, bf16[768,8192]{1,0:T(8,128)(2,1)} %param.8), kind=kOutput, calls=%fused_computation.26 | convolution fusion | flops 6442844160 | bytes 21757952 | tf_op jit(solution)/shard_map/dot_general | solution.py:70
  274.4 2.9 reshape.59
  277.3 10.3 %convolution_bitcast_fusion = f32[8,256,6,1,128]{4,1,2,0,3:T(8,128)} fusion(bf16[8,64,6,128]{3,2,1,0:T(8,128)(2,1)} %reshape.59, f32[8,6,64]{2,1,0:T(8,128)S(1)} %get-tuple-element.4, f32[8,6,256,64]{2,3,1,0:T(8,128)S(1)} %fusion.4), kind=kOutput, calls=%fused_computation.20 | convolution fusion | flops 205262080 | bytes 10235904 | tf_op jit(solution)/shard_map/chqk,cqhd->ckhd/dot_general | solution.py:77
  287.6 7.2 %multiply_reduce_fusion = (f32[8,6,64]{2,1,0:T(8,128)S(1)}, f32[8,6,64,256]{3,2,1,0:T(8,128)}) fusion(f32[8,6,64,256]{3,2,1,0:T(8,128)} %get-tuple-element.5, f32[8,6,64]{2,1,0:T(8,128)S(1)} %get-tuple-element.4, bf16[8,256,6,1,128]{4,3,2,1,0:T(2,128)(2,1)} %get-tuple-element.3, bf16[8,64,6,128]{3,2,1,0:T(8,128)(2,1)} %reshape.59), kind=kOutput, calls=%fused_computation.18 | convolution fusion | flops 203682816 | bytes 10248192 | tf_op jit(solution)/shard_map/cqhd,ckhd->chqk/dot_general | solution.py:80
  294.8 11.7 %multiply_bitcast_fusion = f32[8,256,6,1,128]{4,1,2,0,3:T(8,128)} fusion(f32[8,6,64,256]{3,2,1,0:T(8,128)} %get-tuple-element.7, f32[8,6,64]{2,1,0:T(8,128)S(1)} %get-tuple-element.6, bf16[8,64,6,128]{3,2,1,0:T(8,128)(2,1)} %reshape.57, f32[8,6,64]{2,1,0:T(8,128)S(1)} %get-tuple-element.4, f32[8,6,256,64]{2,3,1,0:T(8,128)S(1)} %fusion.4), kind=kOutput, calls=%fused_computation.9 | convolution fusion | flops 208407808 | bytes 13393920 | tf_op jit(solution)/shard_map/chqk,cqhd->ckhd/dot_general | solution.py:86
  306.5 10.9 %pad_maximum_fusion = f32[8,256,6,2,128]{4,1,2,0,3:T(8,128)} fusion(f32[8,256,6,1,128]{4,1,2,0,3:T(8,128)} %convolution_bitcast_fusion, f32[8,256,6,1,128]{4,1,2,0,3:T(8,128)} %multiply_bitcast_fusion), kind=kLoop, calls=%fused_computation.5 | loop fusion | flops 3145728 | bytes 25165824 | tf_op jit(solution)/shard_map/stack | solution.py:89
  317.4 22.2 %copy.84 = f32[8,256,6,2,128]{4,3,2,1,0:T(2,128)} copy(f32[8,256,6,2,128]{4,1,2,0,3:T(8,128)} %pad_maximum_fusion) | data formatting | bytes 25165824 | tf_op jit(solution)/shard_map/stack | solution.py:89
  339.6 21.3 %reshape.60 = f32[16,196608]{1,0:T(8,128)} reshape(f32[8,256,6,2,128]{4,3,2,1,0:T(2,128)} %copy.84) | data formatting | bytes 25165824 | tf_op jit(solution)/shard_map/reshape | solution.py:89
  360.9 10.9 %fusion.1 = bf16[16,1,196608]{2,0,1:T(8,128)(2,1)} fusion(f32[16,196608]{1,0:T(8,128)} %reshape.60, s32[16]{0:T(128)S(1)} %reshape.53), kind=kOutput, calls=%fused_computation.3 | convolution fusion | flops 607125760 | bytes 18874432 | tf_op jit(solution)/shard_map/dot_general | solution.py:90
  371.8 0.5 broadcast.20
  372.3 8.8 %reduce.4 = bf16[16,196608]{1,0:T(8,128)(2,1)} reduce(bf16[16,1,196608]{2,0,1:T(8,128)(2,1)} %fusion.1, bf16[]{:T(256)} %broadcast.20), dimensions={1}, to_apply=%copy.85.reduce_sub_computation | reduce | bytes 12582914 | tf_op jit(solution)/shard_map/all_to_all | solution.py:97
  381.2 9.3 %reshape.67 = bf16[16,2,98304]{2,1,0:T(2,128)(2,1)} reshape(bf16[16,196608]{1,0:T(8,128)(2,1)} %reduce.4) | data formatting | bytes 12582912
  390.5 7.2 %all-to-all-start = ((bf16[16,2,98304]{2,1,0:T(2,128)(2,1)}), bf16[16,2,98304]{2,1,0:T(2,128)(2,1)}, u32[]{:S(2)}, u32[]{:S(2)}) async-start(bf16[16,2,98304]{2,1,0:T(2,128)(2,1)} %reshape.67), calls=%async_computation.1 | async-start | bytes 12582912 | tf_op jit(solution)/shard_map/all_to_all | solution.py:97
  397.7 0.1 copy.79
  397.9 0.1 copy.78
  398.0 0.1 broadcast_in_dim.14
  398.1 0.1 eq.60
  398.1 0.2 select_reduce_fusion
  398.3 0.2 dynamic-slice_reduce_fusion
  398.5 0.1 fusion.22
  398.6 0.2 dynamic-slice_reduce_fusion.1
  398.8 107.1 %all-to-all-done = bf16[16,2,98304]{2,1,0:T(2,128)(2,1)} async-done(((bf16[16,2,98304]{2,1,0:T(2,128)(2,1)}), bf16[16,2,98304]{2,1,0:T(2,128)(2,1)}, u32[]{:S(2)}, u32[]{:S(2)}) %all-to-all-start) | async-done | bytes 6291488 | tf_op jit(solution)/shard_map/all_to_all | solution.py:97
  505.9 14.3 %reshape.68 = bf16[16,1,196608]{2,1,0:T(2,128)(2,1)} reshape(bf16[16,2,98304]{2,1,0:T(2,128)(2,1)} %all-to-all-done) | data formatting | bytes 12582912
  520.2 12.8 %convolution_convert_fusion.2 = bf16[2,196608]{1,0:T(2,128)(2,1)S(1)} fusion(bf16[16,1,196608]{2,1,0:T(2,128)(2,1)} %reshape.68, s32[16]{0:T(128)S(1)} %dynamic-slice_reduce_fusion, pred[16]{0:T(512)(128)(4,1)S(1)} %dynamic-slice_reduce_fusion.1), kind=kOutput, calls=%fused_computation.4 | convolution fusion | flops 12976192 | bytes 7077968 | tf_op jit(solution)/shard_map/dot_general | solution.py:98
  533.1 1.6 reshape.61
  (15 shorter events, 0.2 us)
Async XLA Ops:
  7.2 89.8 %all-reduce.2.cloned.1.call-start = ((), (), s32[]{:S(2)}) async-start(), calls=%async_computation.2 | async-start | bytes 12582912 | tf_op jit(solution)/shard_map/psum | solution.py:22
  7.9 92.6 %copy-start.2 = (s32[128,2]{0,1:T(2,128)S(1)}, s32[128,2]{0,1:T(2,128)}, u32[]{:S(2)}) copy-start(s32[128,2]{0,1:T(2,128)} %param.11) | copy-start | bytes 3076
  7.9 92.6 %copy-start.3 = (s32[128,2]{0,1:T(2,128)S(1)}, s32[128,2]{0,1:T(2,128)}, u32[]{:S(2)}) copy-start(s32[128,2]{0,1:T(2,128)} %param.10) | copy-start | bytes 3076
  7.9 93.0 %copy-start.1 = (bf16[512,768]{1,0:T(8,128)(2,1)S(1)}, bf16[512,768]{1,0:T(8,128)(2,1)}, u32[]{:S(2)}) copy-start(bf16[512,768]{1,0:T(8,128)(2,1)} %param.7) | copy-start | bytes 2359300
  7.9 179.8 %all-gather.6.cloned.1.call-start = ((), (), s32[]{:S(2)}) async-start(), calls=%async_computation.5 | async-start | bytes 13369344 | tf_op jit(solution)/shard_map/all_gather | solution.py:45
  99.7 161.2 %all-gather.4.cloned.1.call-start = ((), (), s32[]{:S(2)}) async-start(), calls=%async_computation.4 | async-start | bytes 9437184 | tf_op jit(solution)/shard_map/all_gather | solution.py:71
  100.4 434.3 %reduce-scatter.2.cloned.1.call-start = ((), (), s32[]{:S(2)}) async-start(), calls=%async_computation.3 | async-start | bytes 9437184 | tf_op jit(solution)/shard_map/reduce_scatter | solution.py:67
  219.3 13.7 %copy-start = (bf16[8,64,6,128]{3,2,1,0:T(8,128)(2,1)S(1)}, bf16[8,64,6,128]{3,2,1,0:T(8,128)(2,1)}, u32[]{:S(2)}) copy-start(bf16[8,64,6,128]{3,2,1,0:T(8,128)(2,1)} %reshape.57) | copy-start | bytes 2359300
  390.5 115.4 %all-to-all-start = ((bf16[16,2,98304]{2,1,0:T(2,128)(2,1)}), bf16[16,2,98304]{2,1,0:T(2,128)(2,1)}, u32[]{:S(2)}, u32[]{:S(2)}) async-start(bf16[16,2,98304]{2,1,0:T(2,128)(2,1)} %reshape.67), calls=%async_computation.1 | async-start | bytes 12582912 | tf_op jit(solution)/shard_map/all_to_all | solution.py:97
Sparse Core Ops, SparseCore 0:
  10.4 86.5 all-reduce.1
  99.8 87.8 all-gather.5
  189.4 51.1 all-gather.3
  261.0 53.9 reduce-scatter.1
where the time goes:
time: 549 us; the launch traced here: 541 us
  waiting for transfers between devices  283 us (52%)
  local copies, waits for them, and re-layouts  113 us (21%)
  matrix products  101 us (18%)
  other arithmetic  23.6 us (4%)
  between operations  14.1 us (3%)
  starting transfers between devices  7.38 us (1%)
    all_to_all x1, waiting for transfers between devices, local(): lax.all_to_all(per_owner, 'dp', split_axis=0, concat_axis=0, tiled=True)  107 us
    psum x1, waiting for transfers between devices, local(): summed = lax.psum(local_partial, 'tensor').astype(jnp.float32)  89 us
    all_gather x1, waiting for transfers between devices, local(): everyone = lax.all_gather(share_blocks, 'dp', axis=0, tiled=True)  85 us
    unnamed x14, local copies, waits for them, and re-layouts  36.7 us
    another operation x1, local copies, waits for them, and re-layouts, local(): jnp.stack([grad_keys, grad_values], axis=3).reshape(read_count, block_width)  22.2 us
    reshape x1, local copies, waits for them, and re-layouts, local(): jnp.stack([grad_keys, grad_values], axis=3).reshape(read_count, block_width)  21.3 us
    slice x1, local copies, waits for them, and re-layouts, local(): keys = layout[:, :, :, 0]  13.7 us
    dot_general x1, matrix products, local(): lax.dot_general(lax.all_gather(d_out, 'tensor', axis=1, tiled=True), w_ou...  13.5 us
  transfers between devices with their start and end apart: 5, of which 3 were waited for; matrix products, arithmetic and copies ran while one was open for 43% of the time, Pallas kernels for 0%

commit v1 on v0

--- a/solution.py
+++ b/solution.py
@@ -7,6 +7,13 @@
 SPAN = 64
 NBR_LEN = 128
 NB_DEV = 2
+
+
+def exchange_gather(shard, mesh_axis, along):
+    size = lax.axis_size(mesh_axis)
+    pieces = jnp.stack([shard for _ in range(size)])
+    pieces = lax.all_to_all(pieces, mesh_axis, split_axis=0, concat_axis=0)
+    return jnp.concatenate(pieces, axis=along)
 
 
 def local(kv_part, queries, w_out, d_out, nbr_owner, nbr_slot):
@@ -42,7 +49,7 @@
     owner_select = ((serving_slot[:, None] == slot_ids[None, :]) & serving[:, None]).astype(
         jnp.bfloat16
     )
-    everyone = lax.all_gather(share_blocks, "dp", axis=0, tiled=True)
+    everyone = exchange_gather(share_blocks, "dp", 0)
     wanted = (my_owner * NB_DEV + my_slot)[:, None] == jnp.arange(
         dp_count * NB_DEV, dtype=jnp.int32
     )[None, :]

time: 549 us -> 716 us (1.30)
  the two profiles are of different devices: /device:TPU:28 before, /device:TPU:60 now
where the time goes in v1:
time: 716 us; the launch traced here: 708 us
  waiting for transfers between devices  433 us (60%)
  local copies, waits for them, and re-layouts  123 us (17%)
  matrix products  99.3 us (14%)
  other arithmetic  23.7 us (3%)
  starting transfers between devices  14.4 us (2%)
  between operations  14 us (2%)
    all_to_all x1, waiting for transfers between devices, exchange_gather(): pieces = lax.all_to_all(pieces, mesh_axis, split_axis=0, concat_axis=0)  236 us
    all_to_all x1, waiting for transfers between devices, local(): lax.all_to_all(per_owner, 'dp', split_axis=0, concat_axis=0, tiled=True)  109 us
    psum x1, waiting for transfers between devices, local(): summed = lax.psum(local_partial, 'tensor').astype(jnp.float32)  86.3 us
    unnamed x12, local copies, waits for them, and re-layouts  23.9 us
    another operation x1, local copies, waits for them, and re-layouts, local(): jnp.stack([grad_keys, grad_values], axis=3).reshape(read_count, block_width)  22.2 us
    reshape x1, local copies, waits for them, and re-layouts, local(): jnp.stack([grad_keys, grad_values], axis=3).reshape(read_count, block_width)  21.3 us
  transfers between devices with their start and end apart: 5, of which 3 were waited for; matrix products, arithmetic and copies ran while one was open for 33% of the time, Pallas kernels for 0%

profile of v1, /device:TPU:60, one launch (start us, length us, event | category | flops | bytes accessed | tf_op | source)
XLA Modules:
  0.0 707.8 jit_solution(16700150028126672610)
XLA Ops:
  7.2 0.7 all-reduce.2.cloned.1.call-update
  7.9 86.3 %all-reduce.2.cloned.1.call-done = bf16[256,12288]{1,0:T(8,128)(2,1)} async-done(((bf16[256,12288]{1,0:T(8,128)(2,1)}), bf16[256,12288]{1,0:T(8,128)(2,1)}) %all-reduce.2.cloned.1.call-update) | async-done | bytes 6291472 | tf_op jit(solution)/shard_map/psum | solution.py:29
  94.2 1.2 convert_convert_fusion
  95.3 0.6 stack_reshape.2
  95.9 10.9 %stack.12 = bf16[16,2,196608]{2,1,0:T(2,128)(2,1)} broadcast(bf16[2,196608]{1,0:T(2,128)(2,1)S(1)} %stack_reshape.2), dimensions={1,2} | broadcast | bytes 13369344 | tf_op jit(solution)/shard_map/stack | solution.py:14
  106.8 7.3 %all-to-all-start = ((bf16[16,2,196608]{2,1,0:T(2,128)(2,1)}), bf16[16,2,196608]{2,1,0:T(2,128)(2,1)}, u32[]{:S(2)}, u32[]{:S(2)}) async-start(bf16[16,2,196608]{2,1,0:T(2,128)(2,1)} %stack.12), calls=%async_computation | async-start | bytes 25165824 | tf_op jit(solution)/shard_map/all_to_all | solution.py:15
  114.2 0.7 all-gather.2.cloned.1.call-update
  115.0 0.1 constant_dynamic-slice_fusion
  115.1 0.1 copy.73
  115.2 0.1 reshape.56
  115.2 0.1 copy.72
  115.3 0.1 reshape.55
  115.4 1.9 reshape.59
  117.3 236.4 %all-to-all-done = bf16[16,2,196608]{2,1,0:T(2,128)(2,1)} async-done(((bf16[16,2,196608]{2,1,0:T(2,128)(2,1)}), bf16[16,2,196608]{2,1,0:T(2,128)(2,1)}, u32[]{:S(2)}, u32[]{:S(2)}) %all-to-all-start) | async-done | bytes 12582944 | tf_op jit(solution)/shard_map/all_to_all | solution.py:15
  353.6 11.3 %reshape.57 = bf16[32,196608]{1,0:T(8,128)(2,1)} reshape(bf16[16,2,196608]{2,1,0:T(2,128)(2,1)} %all-to-all-done) | data formatting | bytes 25165824 | tf_op jit(solution)/shard_map/reshape | solution.py:16
  364.9 9.1 %convolution_convert_fusion.1 = bf16[16,196608]{1,0:T(8,128)(2,1)} fusion(bf16[32,196608]{1,0:T(8,128)(2,1)} %reshape.57, s32[16]{0:T(128)S(1)} %multiply_add_fusion), kind=kOutput, calls=%fused_computation.2 | convolution fusion | flops 204472832 | bytes 18874432 | tf_op jit(solution)/shard_map/dot_general | solution.py:56
  374.1 9.8 %reshape.58 = bf16[8,256,6,2,128]{4,3,2,1,0:T(2,128)(2,1)} reshape(bf16[16,196608]{1,0:T(8,128)(2,1)} %convolution_convert_fusion.1) | data formatting | bytes 12582912 | tf_op jit(solution)/shard_map/reshape | solution.py:59
  383.9 13.7 %fusion.42 = (bf16[8,256,6,1,128]{4,3,2,1,0:T(2,128)(2,1)S(1)}, bf16[8,256,6,1,128]{4,3,2,1,0:T(2,128)(2,1)}) fusion(bf16[8,256,6,2,128]{4,3,2,1,0:T(2,128)(2,1)} %reshape.58), kind=kLoop, calls=%fused_computation.54 | loop fusion | bytes 12582912 | tf_op jit(solution)/shard_map/slice | solution.py:60
  397.6 1.2 fusion.4
  398.8 2.3 fusion.43
  401.1 9.1 %fusion.12 = bf16[8,64,6,128]{3,1,2,0:T(8,128)(2,1)} fusion(bf16[8,256,6,1,128]{4,3,2,1,0:T(2,128)(2,1)} %get-tuple-element.3, f32[8,6,64]{2,1,0:T(8,128)S(1)} %get-tuple-element.4, f32[8,6,256,64]{2,3,1,0:T(8,128)S(1)} %fusion.4), kind=kOutput, calls=%fused_computation.27 | convolution fusion | flops 205655296 | bytes 7090176 | tf_op jit(solution)/shard_map/chqk,ckhd->cqhd/dot_general | solution.py:71
  410.3 1.7 copy.77
  411.9 13.4 %convolution_convert_fusion.3 = bf16[512,8192]{1,0:T(8,128)(2,1)} fusion(bf16[768,8192]{1,0:T(8,128)(2,1)} %param.8, bf16[64,8,6,128]{3,2,1,0:T(8,128)(2,1)S(1)} %bitcast.71), kind=kOutput, calls=%fused_computation.6 | convolution fusion | flops 6446645248 | bytes 21757952 | tf_op jit(solution)/shard_map/dot_general | solution.py:73
  425.4 13.5 %convolution_convert_fusion.5 = bf16[512,768]{1,0:T(8,128)(2,1)} fusion(bf16[512,8192]{1,0:T(8,128)(2,1)} %all-gather.2.cloned.1.call-done, bf16[768,8192]{1,0:T(8,128)(2,1)} %param.8), kind=kOutput, calls=%fused_computation.26 | convolution fusion | flops 6442844160 | bytes 21757952 | tf_op jit(solution)/shard_map/dot_general | solution.py:77
  438.9 2.9 reshape.61
  441.9 10.3 %convolution_bitcast_fusion = f32[8,256,6,1,128]{4,1,2,0,3:T(8,128)} fusion(bf16[8,64,6,128]{3,2,1,0:T(8,128)(2,1)} %reshape.61, f32[8,6,64]{2,1,0:T(8,128)S(1)} %get-tuple-element.4, f32[8,6,256,64]{2,3,1,0:T(8,128)S(1)} %fusion.4), kind=kOutput, calls=%fused_computation.20 | convolution fusion | flops 205262080 | bytes 10235904 | tf_op jit(solution)/shard_map/chqk,cqhd->ckhd/dot_general | solution.py:84
  452.1 7.2 %multiply_reduce_fusion = (f32[8,6,64]{2,1,0:T(8,128)S(1)}, f32[8,6,64,256]{3,2,1,0:T(8,128)}) fusion(f32[8,6,64,256]{3,2,1,0:T(8,128)} %get-tuple-element.5, f32[8,6,64]{2,1,0:T(8,128)S(1)} %get-tuple-element.4, bf16[8,256,6,1,128]{4,3,2,1,0:T(2,128)(2,1)} %get-tuple-element.3, bf16[8,64,6,128]{3,2,1,0:T(8,128)(2,1)} %reshape.61), kind=kOutput, calls=%fused_computation.18 | convolution fusion | flops 203682816 | bytes 10248192 | tf_op jit(solution)/shard_map/cqhd,ckhd->chqk/dot_general | solution.py:87
  459.4 11.7 %multiply_bitcast_fusion = f32[8,256,6,1,128]{4,1,2,0,3:T(8,128)} fusion(f32[8,6,64,256]{3,2,1,0:T(8,128)} %get-tuple-element.7, f32[8,6,64]{2,1,0:T(8,128)S(1)} %get-tuple-element.6, bf16[8,64,6,128]{3,2,1,0:T(8,128)(2,1)} %reshape.59, f32[8,6,64]{2,1,0:T(8,128)S(1)} %get-tuple-element.4, f32[8,6,256,64]{2,3,1,0:T(8,128)S(1)} %fusion.4), kind=kOutput, calls=%fused_computation.9 | convolution fusion | flops 208407808 | bytes 13393920 | tf_op jit(solution)/shard_map/chqk,cqhd->ckhd/dot_general | solution.py:93
  471.1 11.0 %pad_maximum_fusion = f32[8,256,6,2,128]{4,1,2,0,3:T(8,128)} fusion(f32[8,256,6,1,128]{4,1,2,0,3:T(8,128)} %convolution_bitcast_fusion, f32[8,256,6,1,128]{4,1,2,0,3:T(8,128)} %multiply_bitcast_fusion), kind=kLoop, calls=%fused_computation.5 | loop fusion | flops 3145728 | bytes 25165824 | tf_op jit(solution)/shard_map/stack | solution.py:96
  482.1 22.2 %copy.84 = f32[8,256,6,2,128]{4,3,2,1,0:T(2,128)} copy(f32[8,256,6,2,128]{4,1,2,0,3:T(8,128)} %pad_maximum_fusion) | data formatting | bytes 25165824 | tf_op jit(solution)/shard_map/stack | solution.py:96
  504.2 21.3 %reshape.62 = f32[16,196608]{1,0:T(8,128)} reshape(f32[8,256,6,2,128]{4,3,2,1,0:T(2,128)} %copy.84) | data formatting | bytes 25165824 | tf_op jit(solution)/shard_map/reshape | solution.py:96
  525.5 10.9 %fusion.1 = bf16[16,1,196608]{2,0,1:T(8,128)(2,1)} fusion(f32[16,196608]{1,0:T(8,128)} %reshape.62, s32[16]{0:T(128)S(1)} %reshape.55), kind=kOutput, calls=%fused_computation.3 | convolution fusion | flops 607125760 | bytes 18874432 | tf_op jit(solution)/shard_map/dot_general | solution.py:97
  536.4 0.5 broadcast.21
  537.0 8.8 %reduce.4 = bf16[16,196608]{1,0:T(8,128)(2,1)} reduce(bf16[16,1,196608]{2,0,1:T(8,128)(2,1)} %fusion.1, bf16[]{:T(256)} %broadcast.21), dimensions={1}, to_apply=%copy.85.reduce_sub_computation | reduce | bytes 12582914 | tf_op jit(solution)/shard_map/all_to_all | solution.py:104
  545.8 9.3 %reshape.66 = bf16[16,2,98304]{2,1,0:T(2,128)(2,1)} reshape(bf16[16,196608]{1,0:T(8,128)(2,1)} %reduce.4) | data formatting | bytes 12582912
  555.2 6.9 all-to-all-start.1
  562.1 0.1 copy.79
  562.2 0.1 copy.78
  562.3 0.1 broadcast_in_dim.14
  562.4 0.1 eq.60
  562.5 0.2 select_reduce_fusion
  562.6 0.2 dynamic-slice_reduce_fusion
  562.8 0.1 fusion.22
  563.0 0.2 dynamic-slice_reduce_fusion.1
  563.1 109.2 %all-to-all-done.1 = bf16[16,2,98304]{2,1,0:T(2,128)(2,1)} async-done(((bf16[16,2,98304]{2,1,0:T(2,128)(2,1)}), bf16[16,2,98304]{2,1,0:T(2,128)(2,1)}, u32[]{:S(2)}, u32[]{:S(2)}) %all-to-all-start.1) | async-done | bytes 6291488 | tf_op jit(solution)/shard_map/all_to_all | solution.py:104
  672.3 14.3 %reshape.67 = bf16[16,1,196608]{2,1,0:T(2,128)(2,1)} reshape(bf16[16,2,98304]{2,1,0:T(2,128)(2,1)} %all-to-all-done.1) | data formatting | bytes 12582912
  686.6 12.8 %convolution_convert_fusion.2 = bf16[2,196608]{1,0:T(2,128)(2,1)S(1)} fusion(bf16[16,1,196608]{2,1,0:T(2,128)(2,1)} %reshape.67, s32[16]{0:T(128)S(1)} %dynamic-slice_reduce_fusion, pred[16]{0:T(512)(128)(4,1)S(1)} %dynamic-slice_reduce_fusion.1), kind=kOutput, calls=%fused_computation.4 | convolution fusion | flops 12976192 | bytes 7077968 | tf_op jit(solution)/shard_map/dot_general | solution.py:105
  699.5 1.6 reshape.63
  (15 shorter events, 0.2 us)
Async XLA Ops:
  7.2 87.0 %all-reduce.2.cloned.1.call-start = ((), (), s32[]{:S(2)}) async-start(), calls=%async_computation.3 | async-start | bytes 12582912 | tf_op jit(solution)/shard_map/psum | solution.py:29
  106.8 8.2 %copy-start.2 = (s32[128,2]{0,1:T(2,128)S(1)}, s32[128,2]{0,1:T(2,128)}, u32[]{:S(2)}) copy-start(s32[128,2]{0,1:T(2,128)} %param.11) | copy-start | bytes 3076
  106.8 8.2 %copy-start.3 = (s32[128,2]{0,1:T(2,128)S(1)}, s32[128,2]{0,1:T(2,128)}, u32[]{:S(2)}) copy-start(s32[128,2]{0,1:T(2,128)} %param.10) | copy-start | bytes 3076
  106.8 8.6 %copy-start.1 = (bf16[512,768]{1,0:T(8,128)(2,1)S(1)}, bf16[512,768]{1,0:T(8,128)(2,1)}, u32[]{:S(2)}) copy-start(bf16[512,768]{1,0:T(8,128)(2,1)} %param.7) | copy-start | bytes 2359300
  106.8 246.8 %all-to-all-start = ((bf16[16,2,196608]{2,1,0:T(2,128)(2,1)}), bf16[16,2,196608]{2,1,0:T(2,128)(2,1)}, u32[]{:S(2)}, u32[]{:S(2)}) async-start(bf16[16,2,196608]{2,1,0:T(2,128)(2,1)} %stack.12), calls=%async_computation | async-start | bytes 25165824 | tf_op jit(solution)/shard_map/all_to_all | solution.py:15
  114.2 311.2 %all-gather.2.cloned.1.call-start = ((), (), s32[]{:S(2)}) async-start(), calls=%async_computation.5 | async-start | bytes 9437184 | tf_op jit(solution)/shard_map/all_gather | solution.py:78
  114.9 586.1 %reduce-scatter.2.cloned.1.call-start = ((), (), s32[]{:S(2)}) async-start(), calls=%async_computation.4 | async-start | bytes 9437184 | tf_op jit(solution)/shard_map/reduce_scatter | solution.py:74
  383.9 13.7 %copy-start = (bf16[8,64,6,128]{3,2,1,0:T(8,128)(2,1)S(1)}, bf16[8,64,6,128]{3,2,1,0:T(8,128)(2,1)}, u32[]{:S(2)}) copy-start(bf16[8,64,6,128]{3,2,1,0:T(8,128)(2,1)} %reshape.59) | copy-start | bytes 2359300
  555.2 117.2 %all-to-all-start.1 = ((bf16[16,2,98304]{2,1,0:T(2,128)(2,1)}), bf16[16,2,98304]{2,1,0:T(2,128)(2,1)}, u32[]{:S(2)}, u32[]{:S(2)}) async-start(bf16[16,2,98304]{2,1,0:T(2,128)(2,1)} %reshape.66), calls=%async_computation.2 | async-start | bytes 12582912 | tf_op jit(solution)/shard_map/all_to_all | solution.py:104
Sparse Core Ops, SparseCore 0:
  10.4 83.7 all-reduce.1
  116.7 50.5 all-gather.1
  425.5 49.5 reduce-scatter.1
